TPU v7x, 128 devices: a whole 4x4x4 slice. The times are simulated.
128 devices in a mesh: wide: 64 (over z_hi, x, y, core), narrow: 2 (over z_lo).
Axes of the slice: x: 4, y: 4, z: 4 (z_hi: 2, z_lo: 2; z = z_hi * 2 + z_lo), core: 2. Of those that a mesh axis runs over, the one named last changes fastest.
Arguments:
- pair_rep: bfloat16 [2048, 2048, 128], P('wide', 'narrow'), may hold values from -6 to 6
- pair_bins: int32 [2048, 2048], P('wide', 'narrow'), may hold values from 0 to 31
- token_single: bfloat16 [2048, 768], P('wide'), may hold values from -6 to 6
- atom_single: bfloat16 [64, 768, 128], P('wide'), may hold values from -6 to 6
- atom_token: int32 [64, 768], P('wide'), may hold values from 0 to 31, never falling along the last dimension, each value on 1 to 40 neighbouring positions
- init_coords: float32 [3, 64, 768], P(None, 'wide'), may hold values from -8 to 8
- coord_noise: float32 [2, 3, 64, 768], P(None, None, 'wide'), may hold values from -6 to 6
- pair_gate: bfloat16 [128, 256], replicated, may hold values from -0.5 to 0.5
- pair_up: bfloat16 [128, 256], replicated, may hold values from -0.5 to 0.5
- pair_down: bfloat16 [256, 128], replicated, may hold values from -0.375 to 0.375
- bias_proj: bfloat16 [128, 16], replicated, may hold values from -0.5 to 0.5
- bin_bias: float32 [16, 32], replicated, may hold values from -4 to 256
- token_query: bfloat16 [768, 768], replicated, may hold values from -0.21875 to 0.21875
- token_key: bfloat16 [768, 768], replicated, may hold values from -0.21875 to 0.21875
- token_value: bfloat16 [768, 768], replicated, may hold values from -0.21875 to 0.21875
- token_gate: bfloat16 [768, 768], replicated, may hold values from -0.21875 to 0.21875
- token_out: bfloat16 [768, 768], replicated, may hold values from -0.21875 to 0.21875
- coord_in: float32 [3, 128], replicated, may hold values from -3.5 to 3.5
- atom_lift: float32 [128, 768], replicated, may hold values from -0.5 to 0.5
- token_down: bfloat16 [768, 128], replicated, may hold values from -0.21875 to 0.21875
- atom_query: bfloat16 [128, 128], replicated, may hold values from -0.5 to 0.5
- atom_key: bfloat16 [128, 128], replicated, may hold values from -0.5 to 0.5
- atom_value: bfloat16 [128, 128], replicated, may hold values from -0.5 to 0.5
- atom_out: bfloat16 [128, 128], replicated, may hold values from -0.5 to 0.5
- window_bias: float32 [4, 32, 128], replicated, may hold values from -4 to 256
- coord_out: bfloat16 [3, 128], replicated, may hold values from -0.5 to 0.5
Outputs:
- coords: float32 [3, 64, 768], P(None, 'wide')
- token_state: bfloat16 [2048, 768], P('wide')
All inputs are finite; a program needn't handle non-finite values.
Results may differ from a plain program's by a relative error of at most 0.006.
Values may be sent and summed in bfloat16 or wider, within the bound.
A program may use at most 128 MiB of HBM per device.

v0:
```python
import math

import jax
import jax.numpy as jnp
from jax import lax
from jax.sharding import PartitionSpec as P

D_TOK = 768
HEADS = 16
HEAD_DIM = 48
ATOM_HEADS = 4
QWIN = 32
KWIN = 128
STEPS = 2
RIM = 48


EPSILON = 1e-05
HIGHEST = lax.Precision.HIGHEST
MASKED_SCORE = -1e30


def extended(block, sides, width):
    for axis, dim in sides:
        count = lax.axis_size(axis)
        forward = [(i, i + 1) for i in range(count - 1)]
        backward = [(target, source) for source, target in forward]
        low = lax.ppermute(
            lax.slice_in_dim(block, block.shape[dim] - width, None, axis=dim), axis, forward
        )
        high = lax.ppermute(lax.slice_in_dim(block, 0, width, axis=dim), axis, backward)
        block = jnp.concatenate([low, block, high], axis=dim)
    return block


def layer_norm(value):
    centred = value - jnp.mean(value, axis=-1, keepdims=True)
    return centred * lax.rsqrt(jnp.mean(centred * centred, axis=-1, keepdims=True) + EPSILON)


def pair_block_bias(block_pair, block_bins, pair_gate, pair_up, pair_down, bias_proj, bin_bias):
    pair_input = block_pair.astype(jnp.float32)
    normed = layer_norm(pair_input).astype(jnp.bfloat16)
    lift_a = jnp.einsum("rck,kf->rcf", normed, pair_gate, preferred_element_type=jnp.float32)
    lift_b = jnp.einsum("rck,kf->rcf", normed, pair_up, preferred_element_type=jnp.float32)
    hidden = (jax.nn.silu(lift_a) * lift_b).astype(jnp.bfloat16)
    conditioned = pair_input + jnp.einsum(
        "rcf,fk->rck", hidden, pair_down, preferred_element_type=jnp.float32
    )
    cond_normed = layer_norm(conditioned).astype(jnp.bfloat16)
    planes = jnp.einsum("rck,kh->hrc", cond_normed, bias_proj, preferred_element_type=jnp.float32)
    levels = jnp.arange(bin_bias.shape[1], dtype=jnp.int32)
    onehot = (block_bins[None, :, :] == levels[:, None, None]).astype(jnp.float32)
    return planes + jnp.einsum("hb,brc->hrc", bin_bias, onehot, precision=HIGHEST)


def make_absorb(queries, token_bias, head_count, score_scale):
    tok_rows = queries.shape[0]
    query_heads = queries.reshape(tok_rows, head_count, HEAD_DIM)

    def absorb(state_now, pieces, offset):
        running_max, running_sum, weighted = state_now
        key_piece, value_piece = pieces
        piece_rows = key_piece.shape[0]
        key_heads = key_piece.reshape(piece_rows, head_count, HEAD_DIM)
        value_heads = value_piece.reshape(piece_rows, head_count, HEAD_DIM)
        scores = (
            jnp.einsum("qhd,khd->hqk", query_heads, key_heads, preferred_element_type=jnp.float32)
            * score_scale
        )
        scores = scores + token_bias
        new_max = jnp.maximum(running_max, jnp.max(scores, axis=2))
        exponents = jnp.exp(scores - new_max[:, :, None])
        running_sum = jnp.sum(exponents, axis=2)
        weighted = jnp.einsum(
            "hqk,khd->hqd",
            exponents.astype(jnp.bfloat16),
            value_heads,
            preferred_element_type=jnp.float32,
        )
        return (new_max, running_sum, weighted)

    return absorb


def window_attend(query_atoms, padded, window_bias, key_valid):
    atom_rows, channels = query_atoms.shape
    window_count = atom_rows // QWIN
    head_dim = channels // ATOM_HEADS
    window_parts = [
        padded[:, offset * QWIN : offset * QWIN + atom_rows].reshape(
            2, window_count, QWIN, channels
        )
        for offset in range(KWIN // QWIN)
    ]
    windows = jnp.stack(window_parts, axis=2).reshape(2, window_count, KWIN, ATOM_HEADS, head_dim)
    query_win = query_atoms.reshape(window_count, QWIN, ATOM_HEADS, head_dim)
    scores = (
        jnp.einsum("bqhd,bkhd->bhqk", query_win, windows[0], preferred_element_type=jnp.float32)
        * (1.0 / math.sqrt(head_dim))
        + window_bias[None]
    )
    scores = jnp.where(key_valid[:, None, None, :], scores, MASKED_SCORE)
    row_max = jnp.max(scores, axis=3, keepdims=True)
    exponents = jnp.exp(scores - row_max)
    attended = jnp.einsum(
        "bhqk,bkhd->bqhd",
        exponents.astype(jnp.bfloat16),
        windows[1],
        preferred_element_type=jnp.float32,
    )
    totals = jnp.sum(exponents, axis=3)
    attended = attended / jnp.transpose(totals, (0, 2, 1))[:, :, :, None]
    return attended.reshape(atom_rows, channels).astype(jnp.bfloat16)


def local(
    pair_rep,
    pair_bins,
    token_single,
    atom_single,
    atom_token,
    init_coords,
    coord_noise,
    pair_gate,
    pair_up,
    pair_down,
    bias_proj,
    bin_bias,
    token_query,
    token_key,
    token_value,
    token_gate,
    token_out,
    coord_in,
    atom_lift,
    token_down,
    atom_query,
    atom_key,
    atom_value,
    atom_out,
    window_bias,
    coord_out,
):
    tok_rows = token_single.shape[0]
    column_count = pair_rep.shape[1]
    atom_rows = atom_single.shape[1]
    block_rows = 4
    split_pair = pair_rep.reshape(
        tok_rows // block_rows, block_rows, column_count, pair_rep.shape[2]
    )
    split_bins = pair_bins.reshape(tok_rows // block_rows, block_rows, column_count)

    def block_bias(operands):
        return pair_block_bias(
            operands[0], operands[1], pair_gate, pair_up, pair_down, bias_proj, bin_bias
        )

    planes = lax.map(block_bias, (split_pair, split_bins))
    bias_tile = jnp.transpose(planes, (1, 0, 2, 3)).reshape(HEADS, tok_rows, column_count)
    token_bias = lax.all_gather(bias_tile, "narrow", axis=2, tiled=True)
    head_width = D_TOK
    head_count = token_bias.shape[0]
    score_scale = 1.0 / math.sqrt(HEAD_DIM)
    owner_local = atom_token[0]
    onehot = (owner_local[None, :] == jnp.arange(tok_rows, dtype=jnp.int32)[:, None]).astype(
        jnp.float32
    )
    onehot_half = onehot.astype(jnp.bfloat16)
    counts = jnp.sum(onehot, axis=1)
    atom_base = atom_single[0].astype(jnp.float32)
    token_base = token_single.astype(jnp.float32)
    coords = init_coords[:, 0, :]
    atom_first = lax.axis_index("wide") * atom_rows
    atom_all = lax.axis_size("wide") * atom_rows
    window_count = atom_rows // QWIN
    position = (
        atom_first
        + jnp.arange(window_count, dtype=jnp.int32)[:, None] * QWIN
        + jnp.arange(KWIN, dtype=jnp.int32)[None, :]
        - RIM
    )
    key_valid = (position >= 0) & (position < atom_all)
    token_act = token_base
    for denoise_step in range(STEPS):
        sigma_now = 1.5 * 0.65**denoise_step
        sigma_next = 1.5 * 0.65 ** (denoise_step + 1)
        sigma_hat = 1.4 * sigma_now
        noisy_coords = coords + sigma_now * math.sqrt(0.96) * coord_noise[denoise_step][:, 0, :]
        scaled = noisy_coords / math.sqrt(sigma_hat * sigma_hat + 1.0)
        atom_feat = atom_base + jnp.einsum("ka,kc->ac", scaled, coord_in, precision=HIGHEST)
        atom_relu = jnp.maximum(atom_feat, 0.0).astype(jnp.bfloat16)
        pooled = jnp.dot(onehot_half, atom_relu, preferred_element_type=jnp.float32)
        token_act = token_base + jnp.dot(pooled, atom_lift, precision=HIGHEST) / counts[:, None]
        tok_normed = layer_norm(token_act).astype(jnp.bfloat16)
        queries = jnp.dot(tok_normed, token_query, preferred_element_type=jnp.float32).astype(
            jnp.bfloat16
        )
        key_rows = jnp.dot(tok_normed, token_key, preferred_element_type=jnp.float32).astype(
            jnp.bfloat16
        )
        value_rows = jnp.dot(tok_normed, token_value, preferred_element_type=jnp.float32).astype(
            jnp.bfloat16
        )
        gate_open = jax.nn.sigmoid(
            jnp.dot(tok_normed, token_gate, preferred_element_type=jnp.float32)
        )
        absorb = make_absorb(queries, token_bias, head_count, score_scale)
        start_state = (
            jnp.full((head_count, tok_rows), MASKED_SCORE, jnp.float32),
            jnp.zeros((head_count, tok_rows), jnp.float32),
            jnp.zeros((head_count, tok_rows, HEAD_DIM), jnp.float32),
        )
        running_max, running_sum, weighted = absorb(
            start_state,
            (
                lax.all_gather(key_rows, "wide", axis=0, tiled=True),
                lax.all_gather(value_rows, "wide", axis=0, tiled=True),
            ),
            jnp.int32(0),
        )
        mixed_heads = jnp.transpose(weighted / running_sum[:, :, None], (1, 0, 2)).reshape(
            tok_rows, head_width
        )
        gated = (mixed_heads * gate_open).astype(jnp.bfloat16)
        token_act = token_act + jnp.dot(gated, token_out, preferred_element_type=jnp.float32)
        down_normed = layer_norm(token_act).astype(jnp.bfloat16)
        token_feed = jnp.dot(down_normed, token_down, preferred_element_type=jnp.float32)
        atom_feat = atom_feat + jnp.einsum("ta,tc->ac", onehot, token_feed, precision=HIGHEST)
        atom_normed = layer_norm(atom_feat).astype(jnp.bfloat16)
        query_atoms = jnp.dot(atom_normed, atom_query, preferred_element_type=jnp.float32).astype(
            jnp.bfloat16
        )
        key_atoms = jnp.dot(atom_normed, atom_key, preferred_element_type=jnp.float32).astype(
            jnp.bfloat16
        )
        value_atoms = jnp.dot(atom_normed, atom_value, preferred_element_type=jnp.float32).astype(
            jnp.bfloat16
        )
        padded = extended(jnp.stack([key_atoms, value_atoms]), (("wide", 1),), RIM)
        atom_mixed = window_attend(query_atoms, padded, window_bias, key_valid)
        atom_feat = atom_feat + jnp.dot(atom_mixed, atom_out, preferred_element_type=jnp.float32)
        final_normed = layer_norm(atom_feat).astype(jnp.bfloat16)
        coord_update = lax.dot_general(
            coord_out, final_normed, (((1,), (1,)), ((), ())), preferred_element_type=jnp.float32
        )
        denoised = (
            noisy_coords / (sigma_hat * sigma_hat + 1.0)
            + sigma_hat / math.sqrt(sigma_hat * sigma_hat + 1.0) * coord_update
        )
        coords = noisy_coords + 1.5 * (sigma_next - sigma_hat) / sigma_hat * (
            noisy_coords - denoised
        )
    return (coords[:, None, :], token_act.astype(jnp.bfloat16))


def solution(mesh):
    placed = (
        P("wide", "narrow", None),
        P("wide", "narrow"),
        P("wide", None),
        P("wide", None, None),
        P("wide", None),
        P(None, "wide", None),
        P(None, None, "wide", None),
        P(),
        P(),
        P(),
        P(),
        P(),
        P(),
        P(),
        P(),
        P(),
        P(),
        P(),
        P(),
        P(),
        P(),
        P(),
        P(),
        P(),
        P(),
        P(),
    )
    return jax.shard_map(
        local,
        mesh=mesh,
        in_specs=placed,
        out_specs=(P(None, "wide", None), P("wide", None)),
        check_vma=False,
    )
```

profile of v0, /device:TPU:1, one launch (start us, length us, event | category | flops | bytes accessed | tf_op | source)
XLA Modules:
  0.0 507.6 jit_solution(10150834307207970074)
XLA Ops:
  16.1 12.0 %copy.89 = bf16[32,1024,128]{1,2,0:T(8,128)(2,1)} copy(bf16[32,1024,128]{2,1,0:T(8,128)(2,1)} %param.28) | data formatting | bytes 16777216 | tf_op args[0]
  28.9 109.9 %while.10 = (s32[]{:T(128)}, f32[8,16,4,1024]{3,1,2,0:T(8,128)}, bf16[8,4,1024,128]{2,3,1,0:T(8,128)(2,1)}, bf16[128,256]{1,0:T(8,128)(2,1)}, bf16[128,256]{1,0:...) while((s32[]{:T(128)}, f32[8,16,4,1024]{3,1,2,0:T(8,128)}, ...), condition=%wide.region_8.9_spmd, body=%wide.region_3.8_spmd.sunk | while | flops 865804288 | bytes 21290112 | solution.py:159
  32.0 4.0 fusion.236
  35.9 5.1 %fusion.237 = (f32[4,1024]{1,0:T(4,128)S(1)}, f32[4,1024,128]{1,2,0:T(8,128)S(1)}) fusion(bf16[256,128]{0,1:T(8,128)(2,1)} %get-tuple-element.237, f32[4,1024,256]{2,1,0:T(8,128)} %fusion.236, f32[4,1024]{1,0:T(4,128)S(1)} %add_rsqrt_fusion.12, f32[4,1024]{1,0:T(4,128)S(1)} %broadcast_multiply_fusion.12, ...), kind=kOutput, calls=%fused_computation.224.clone.1 | convolution fusion | flops 546828288 | bytes 8569856 | tf_op jit(solution)/shard_map/while/body/eval_jaxpr/rcf,fk->rck/dot_general | solution.py:47
  45.7 4.0 fusion.236
  49.6 5.1 %fusion.237 = (f32[4,1024]{1,0:T(4,128)S(1)}, f32[4,1024,128]{1,2,0:T(8,128)S(1)}) fusion(bf16[256,128]{0,1:T(8,128)(2,1)} %get-tuple-element.237, f32[4,1024,256]{2,1,0:T(8,128)} %fusion.236, f32[4,1024]{1,0:T(4,128)S(1)} %add_rsqrt_fusion.12, f32[4,1024]{1,0:T(4,128)S(1)} %broadcast_multiply_fusion.12, ...), kind=kOutput, calls=%fused_computation.224.clone.1 | convolution fusion | flops 546828288 | bytes 8569856 | tf_op jit(solution)/shard_map/while/body/eval_jaxpr/rcf,fk->rck/dot_general | solution.py:47
  59.4 4.0 fusion.236
  63.4 5.1 %fusion.237 = (f32[4,1024]{1,0:T(4,128)S(1)}, f32[4,1024,128]{1,2,0:T(8,128)S(1)}) fusion(bf16[256,128]{0,1:T(8,128)(2,1)} %get-tuple-element.237, f32[4,1024,256]{2,1,0:T(8,128)} %fusion.236, f32[4,1024]{1,0:T(4,128)S(1)} %add_rsqrt_fusion.12, f32[4,1024]{1,0:T(4,128)S(1)} %broadcast_multiply_fusion.12, ...), kind=kOutput, calls=%fused_computation.224.clone.1 | convolution fusion | flops 546828288 | bytes 8569856 | tf_op jit(solution)/shard_map/while/body/eval_jaxpr/rcf,fk->rck/dot_general | solution.py:47
  73.1 4.0 fusion.236
  77.1 5.2 %fusion.237 = (f32[4,1024]{1,0:T(4,128)S(1)}, f32[4,1024,128]{1,2,0:T(8,128)S(1)}) fusion(bf16[256,128]{0,1:T(8,128)(2,1)} %get-tuple-element.237, f32[4,1024,256]{2,1,0:T(8,128)} %fusion.236, f32[4,1024]{1,0:T(4,128)S(1)} %add_rsqrt_fusion.12, f32[4,1024]{1,0:T(4,128)S(1)} %broadcast_multiply_fusion.12, ...), kind=kOutput, calls=%fused_computation.224.clone.1 | convolution fusion | flops 546828288 | bytes 8569856 | tf_op jit(solution)/shard_map/while/body/eval_jaxpr/rcf,fk->rck/dot_general | solution.py:47
  87.0 4.0 fusion.236
  91.0 5.1 %fusion.237 = (f32[4,1024]{1,0:T(4,128)S(1)}, f32[4,1024,128]{1,2,0:T(8,128)S(1)}) fusion(bf16[256,128]{0,1:T(8,128)(2,1)} %get-tuple-element.237, f32[4,1024,256]{2,1,0:T(8,128)} %fusion.236, f32[4,1024]{1,0:T(4,128)S(1)} %add_rsqrt_fusion.12, f32[4,1024]{1,0:T(4,128)S(1)} %broadcast_multiply_fusion.12, ...), kind=kOutput, calls=%fused_computation.224.clone.1 | convolution fusion | flops 546828288 | bytes 8569856 | tf_op jit(solution)/shard_map/while/body/eval_jaxpr/rcf,fk->rck/dot_general | solution.py:47
  100.7 4.0 fusion.236
  104.7 5.1 %fusion.237 = (f32[4,1024]{1,0:T(4,128)S(1)}, f32[4,1024,128]{1,2,0:T(8,128)S(1)}) fusion(bf16[256,128]{0,1:T(8,128)(2,1)} %get-tuple-element.237, f32[4,1024,256]{2,1,0:T(8,128)} %fusion.236, f32[4,1024]{1,0:T(4,128)S(1)} %add_rsqrt_fusion.12, f32[4,1024]{1,0:T(4,128)S(1)} %broadcast_multiply_fusion.12, ...), kind=kOutput, calls=%fused_computation.224.clone.1 | convolution fusion | flops 546828288 | bytes 8569856 | tf_op jit(solution)/shard_map/while/body/eval_jaxpr/rcf,fk->rck/dot_general | solution.py:47
  114.4 4.0 fusion.236
  118.4 5.1 %fusion.237 = (f32[4,1024]{1,0:T(4,128)S(1)}, f32[4,1024,128]{1,2,0:T(8,128)S(1)}) fusion(bf16[256,128]{0,1:T(8,128)(2,1)} %get-tuple-element.237, f32[4,1024,256]{2,1,0:T(8,128)} %fusion.236, f32[4,1024]{1,0:T(4,128)S(1)} %add_rsqrt_fusion.12, f32[4,1024]{1,0:T(4,128)S(1)} %broadcast_multiply_fusion.12, ...), kind=kOutput, calls=%fused_computation.224.clone.1 | convolution fusion | flops 546828288 | bytes 8569856 | tf_op jit(solution)/shard_map/while/body/eval_jaxpr/rcf,fk->rck/dot_general | solution.py:47
  128.1 4.0 fusion.236
  132.1 5.1 %fusion.237 = (f32[4,1024]{1,0:T(4,128)S(1)}, f32[4,1024,128]{1,2,0:T(8,128)S(1)}) fusion(bf16[256,128]{0,1:T(8,128)(2,1)} %get-tuple-element.237, f32[4,1024,256]{2,1,0:T(8,128)} %fusion.236, f32[4,1024]{1,0:T(4,128)S(1)} %add_rsqrt_fusion.12, f32[4,1024]{1,0:T(4,128)S(1)} %broadcast_multiply_fusion.12, ...), kind=kOutput, calls=%fused_computation.224.clone.1 | convolution fusion | flops 546828288 | bytes 8569856 | tf_op jit(solution)/shard_map/while/body/eval_jaxpr/rcf,fk->rck/dot_general | solution.py:47
  138.8 4.1 copy.119
  144.2 1.9 convolution_convert_fusion.9
  147.9 4.7 copy.87
  152.6 52.8 %all-gather.8.cloned.1.call-done = f32[16,32,2048]{2,1,0:T(8,128)} async-done(((f32[16,32,1024]{2,1,0:T(8,128)}), f32[16,32,2048]{2,1,0:T(8,128)}) %all-gather.8.cloned.1.call-update) | async-done | bytes 4194320 | tf_op jit(solution)/shard_map/all_gather | solution.py:161
  205.5 4.2 fusion.165
  209.6 2.0 copy-done.2
  212.3 68.8 %all-gather.10.cloned.1.call-done = bf16[2048,768]{1,0:T(8,128)(2,1)} async-done(((bf16[32,768]{1,0:T(8,128)(2,1)}), bf16[2048,768]{1,0:T(8,128)(2,1)}) %all-gather.10.cloned.1.call-update) | async-done | bytes 3145744 | tf_op jit(solution)/shard_map/all_gather | solution.py:218
  281.2 4.7 copy.92
  285.9 4.3 fusion.74
  292.8 2.0 collective-permute-start
  294.8 2.5 collective-permute-start.1
  300.8 2.8 squeeze.21
  303.6 2.8 squeeze.22
  306.4 3.9 fusion.168
  311.3 1.7 fusion.52
  320.6 2.3 convolution_convert_fusion.6
  322.9 1.6 convolution_convert_fusion.8
  324.8 70.8 %all-gather.12.cloned.1.call-done = bf16[2048,768]{1,0:T(8,128)(2,1)} async-done(((bf16[32,768]{1,0:T(8,128)(2,1)}), bf16[2048,768]{1,0:T(8,128)(2,1)}) %all-gather.12.cloned.1.call-update) | async-done | bytes 3145744 | tf_op jit(solution)/shard_map/all_gather | solution.py:217
  395.6 4.7 copy.103
  400.3 4.2 fusion.171
  404.5 1.9 copy-done.1
  407.1 59.2 %all-gather.14.cloned.1.call-done = bf16[2048,768]{1,0:T(8,128)(2,1)} async-done(((bf16[32,768]{1,0:T(8,128)(2,1)}), bf16[2048,768]{1,0:T(8,128)(2,1)}) %all-gather.14.cloned.1.call-update) | async-done | bytes 3145744 | tf_op jit(solution)/shard_map/all_gather | solution.py:218
  466.3 4.8 copy.105
  471.1 4.3 fusion.71
  478.6 2.0 collective-permute-start.2
  480.6 2.3 collective-permute-start.3
  486.6 2.8 squeeze.23
  489.4 2.8 squeeze.24
  492.2 3.9 fusion.174
  497.1 1.7 fusion.51
  (273 shorter events, 75.1 us)
Async XLA Ops:
  7.2 283.3 %copy-start = (bf16[768,768]{1,0:T(8,128)(2,1)S(1)}, bf16[768,768]{1,0:T(8,128)(2,1)}, u32[]{:S(2)}) copy-start(bf16[768,768]{1,0:T(8,128)(2,1)} %param.44) | copy-start | bytes 3538948
  7.2 7.7 %copy-start.3 = (bf16[768,768]{1,0:T(8,128)(2,1)S(1)}, bf16[768,768]{1,0:T(8,128)(2,1)}, u32[]{:S(2)}) copy-start(bf16[768,768]{1,0:T(8,128)(2,1)} %param.41) | copy-start | bytes 3538948
  7.2 140.7 %all-gather.6.cloned.1.call-start = ((), (), s32[]{:S(2)}) async-start(), calls=%async_computation | async-start | bytes 3194880 | tf_op jit(solution)/shard_map/all_gather | solution.py:217
  8.5 19.7 %copy-start.15 = (bf16[1,768,128]{1,2,0:T(8,128)(2,1)}, bf16[1,768,128]{1,2,0:T(8,128)(2,1)S(1)}, u32[]{:S(2)}) copy-start(bf16[1,768,128]{1,2,0:T(8,128)(2,1)S(1)} %copy.86) | copy-start | bytes 589828
  10.7 5.3 %copy-start.38 = (f32[32]{0:T(128)}, f32[32]{0:T(128)S(1)}, u32[]{:S(2)}) copy-start(f32[32]{0:T(128)S(1)} %convert_reduce_fusion.1) | copy-start | bytes 388
  14.3 1.7 copy-start.34
  15.9 189.5 %all-gather.8.cloned.1.call-start = ((), (), s32[]{:S(2)}) async-start(), calls=%async_computation.1 | async-start | bytes 6291456 | tf_op jit(solution)/shard_map/all_gather | solution.py:161
  16.0 12.1 %copy-start.33 = (bf16[256,128]{1,0:T(8,128)(2,1)S(1)}, bf16[256,128]{1,0:T(8,128)(2,1)}, u32[]{:S(2)}) copy-start(bf16[256,128]{1,0:T(8,128)(2,1)} %param.37) | copy-start | bytes 196612
  16.0 12.8 %copy-start.25 = (s32[32,1024]{1,0:T(8,128)S(1)}, s32[32,1024]{1,0:T(8,128)}, u32[]{:S(2)}) copy-start(s32[32,1024]{1,0:T(8,128)} %param.29) | copy-start | bytes 393220
  16.0 12.8 %copy-start.16 = (bf16[128,256]{1,0:T(8,128)(2,1)S(1)}, bf16[128,256]{1,0:T(8,128)(2,1)}, u32[]{:S(2)}) copy-start(bf16[128,256]{1,0:T(8,128)(2,1)} %param.36) | copy-start | bytes 196612
  16.1 12.8 %copy-start.22 = (f32[16,32]{1,0:T(8,128)S(1)}, f32[16,32]{1,0:T(8,128)}, u32[]{:S(2)}) copy-start(f32[16,32]{1,0:T(8,128)} %param.39) | copy-start | bytes 6148
  16.1 12.8 %copy-start.32 = (bf16[128,16]{0,1:T(8,128)(2,1)S(1)}, bf16[128,16]{0,1:T(8,128)(2,1)}, u32[]{:S(2)}) copy-start(bf16[128,16]{0,1:T(8,128)(2,1)} %param.38) | copy-start | bytes 12292
  142.9 3.4 copy-start.6
  143.0 138.2 %all-gather.10.cloned.1.call-start = ((), (), s32[]{:S(2)}) async-start(), calls=%async_computation.2 | async-start | bytes 3194880 | tf_op jit(solution)/shard_map/all_gather | solution.py:218
  146.1 249.5 %all-gather.12.cloned.1.call-start = ((), (), s32[]{:S(2)}) async-start(), calls=%async_computation.3 | async-start | bytes 3194880 | tf_op jit(solution)/shard_map/all_gather | solution.py:217
  147.9 158.5 %copy-start.41 = (pred[24,128]{1,0:T(8,128)(4,1)}, pred[24,128]{1,0:T(8,128)(4,1)S(1)}, u32[]{:S(2)}) copy-start(pred[24,128]{1,0:T(8,128)(4,1)S(1)} %fusion.140) | copy-start | bytes 9220
  209.6 2.0 copy-start.2
  285.9 4.7 copy-start.7
  285.9 4.7 copy-start.10
  285.9 4.7 copy-start.35
  285.9 4.7 copy-start.37
  290.2 1.6 copy-start.12
  290.5 1.7 copy-start.26
  290.6 2.0 copy-start.28
  291.3 6.0 %copy-start.30 = (bf16[128,128]{1,0:T(8,128)(2,1)S(1)}, bf16[128,128]{1,0:T(8,128)(2,1)}, u32[]{:S(2)}) copy-start(bf16[128,128]{1,0:T(8,128)(2,1)} %param.48) | copy-start | bytes 98308
  292.8 6.0 %collective-permute-start = (bf16[2,48,128]{2,1,0:T(8,128)(2,1)S(1)}, bf16[2,48,128]{2,1,0:T(8,128)(2,1)S(1)}, u32[]{:S(2)}, u32[]{:S(2)}) collective-permute-start(bf16[2,48,128]{2,1,0:T(8,128)(2,1)S(1)} %get-tuple-element.121), channel_id=1, source_target_pairs={{0,2},{2,4},{4,6},{6,8},{8,10},{10,12},{12,14},{14,16},{16,18},{18... | collective-permute-start | bytes 73736 | tf_op jit(solution)/shard_map/ppermute | solution.py:28
  294.8 5.1 %collective-permute-start.1 = (bf16[2,48,128]{2,1,0:T(8,128)(2,1)S(1)}, bf16[2,48,128]{2,1,0:T(8,128)(2,1)S(1)}, u32[]{:S(2)}, u32[]{:S(2)}) collective-permute-start(bf16[2,48,128]{2,1,0:T(8,128)(2,1)S(1)} %get-tuple-element.122), channel_id=1, source_target_pairs={{2,0},{4,2},{6,4},{8,6},{10,8},{12,10},{14,12},{16,14},{18,16},{20... | collective-permute-start | bytes 73736 | tf_op jit(solution)/shard_map/ppermute | solution.py:31
  303.6 2.8 copy-start.21
  303.6 2.8 copy-start.43
  306.4 4.9 copy-start.14
  313.6 5.7 %copy-start.4 = (bf16[768,768]{1,0:T(8,128)(2,1)S(1)}, bf16[768,768]{1,0:T(8,128)(2,1)}, u32[]{:S(2)}) copy-start(bf16[768,768]{1,0:T(8,128)(2,1)} %param.41) | copy-start | bytes 3538948
  314.7 3.9 copy-start.17
  314.7 3.9 copy-start.23
  314.7 3.9 copy-start.39
  320.3 146.0 %all-gather.14.cloned.1.call-start = ((), (), s32[]{:S(2)}) async-start(), calls=%async_computation.4 | async-start | bytes 3194880 | tf_op jit(solution)/shard_map/all_gather | solution.py:218
  404.5 1.9 copy-start.1
  471.1 4.6 copy-start.8
  475.4 1.9 copy-start.19
  475.8 2.3 copy-start.27
  475.8 2.5 copy-start.29
  476.5 6.4 %copy-start.31 = (bf16[128,128]{1,0:T(8,128)(2,1)S(1)}, bf16[128,128]{1,0:T(8,128)(2,1)}, u32[]{:S(2)}) copy-start(bf16[128,128]{1,0:T(8,128)(2,1)} %param.48) | copy-start | bytes 98308
  478.6 5.8 %collective-permute-start.2 = (bf16[2,48,128]{2,1,0:T(8,128)(2,1)S(1)}, bf16[2,48,128]{2,1,0:T(8,128)(2,1)S(1)}, u32[]{:S(2)}, u32[]{:S(2)}) collective-permute-start(bf16[2,48,128]{2,1,0:T(8,128)(2,1)S(1)} %get-tuple-element.117), channel_id=1, source_target_pairs={{0,2},{2,4},{4,6},{6,8},{8,10},{10,12},{12,14},{14,16},{16,18},{18... | collective-permute-start | bytes 73736 | tf_op jit(solution)/shard_map/ppermute | solution.py:28
  480.6 5.1 %collective-permute-start.3 = (bf16[2,48,128]{2,1,0:T(8,128)(2,1)S(1)}, bf16[2,48,128]{2,1,0:T(8,128)(2,1)S(1)}, u32[]{:S(2)}, u32[]{:S(2)}) collective-permute-start(bf16[2,48,128]{2,1,0:T(8,128)(2,1)S(1)} %get-tuple-element.118), channel_id=1, source_target_pairs={{2,0},{4,2},{6,4},{8,6},{10,8},{12,10},{14,12},{16,14},{18,16},{20... | collective-permute-start | bytes 73736 | tf_op jit(solution)/shard_map/ppermute | solution.py:31
  489.4 2.8 copy-start.20
  489.4 2.8 copy-start.42
  489.4 2.8 copy-start.44
  492.2 4.9 copy-start.13
  498.9 1.4 copy-start.40
  (6 other events, 6.1 us)
Sparse Core Ops, SparseCore 0:
  16.1 73.9 all-gather.5
  143.1 62.3 all-gather.7
  209.3 71.8 all-gather.9
  320.5 75.0 all-gather.11
  399.2 67.0 all-gather.13
where the time goes:
time: 514 us; the launch traced here: 508 us
  waiting for transfers between devices  254 us (49%)
  matrix products  132 us (26%)
  local copies, waits for them, and re-layouts  63.8 us (12%)
  other arithmetic  33 us (6%)
  between operations  14.7 us (3%)
  starting transfers between devices  9.51 us (2%)
    all_gather x2, waiting for transfers between devices, local(): lax.all_gather(value_rows, 'wide', axis=0, tiled=True)  128 us
    all_gather x2, waiting for transfers between devices, local(): lax.all_gather(key_rows, 'wide', axis=0, tiled=True)  70.9 us
    all_gather x1, waiting for transfers between devices, local(): token_bias = lax.all_gather(bias_tile, 'narrow', axis=2, tiled=True)  52.8 us
    dot_general x8, matrix products, pair_block_bias(): jnp.einsum('rcf,fk->rck', hidden, pair_down, preferred_element_type=jnp.f...  41 us
    dot_general x8, matrix products, pair_block_bias(): jnp.einsum('rck,kf->rcf', normed, pair_up, preferred_element_type=jnp.flo...  31.6 us
    unnamed x93, local copies, waits for them, and re-layouts  20.3 us
    reduce_sum x23, other arithmetic, layer_norm(): jnp.mean(centred * centred, axis=-1, keepdims=True) + EPSILON  15.3 us
    reduce_sum x8, other arithmetic, layer_norm(): centred = value - jnp.mean(value, axis=-1, keepdims=True)  11.5 us
  transfers between devices with their start and end apart: 9, of which 6 were waited for; matrix products, arithmetic and copies ran while one was open for 31% of the time, Pallas kernels for 0%

commit v1 on v0

v1 whole, which is shorter than its diff:
```python
import math

import jax
import jax.numpy as jnp
from jax import lax
from jax.experimental import pallas as pl
from jax.experimental.pallas import tpu as pltpu
from jax.sharding import PartitionSpec as P

D_TOK = 768
HEADS = 16
HEAD_DIM = 48
CZ = 128
FF_Z = 256
C_ATOM = 128
ATOM_HEADS = 4
ATOM_DIM = C_ATOM // ATOM_HEADS
QWIN = 32
KWIN = 128
NBIN = 32
STEPS = 2
RIM = 48
EPSILON = 1e-05
MASKED_SCORE = -1e30
PAIR_COLS = 256

F32 = jnp.float32
BF16 = jnp.bfloat16
HIGHEST = lax.Precision.HIGHEST
MESH = pl.DeviceIdType.MESH


def nt(a, b):
    return lax.dot_general(a, b, (((1,), (1,)), ((), ())), preferred_element_type=F32)


def nn(a, b):
    return jnp.dot(a, b, preferred_element_type=F32)


def iota(shape, dim):
    return lax.broadcasted_iota(jnp.int32, shape, dim)


def layer_norm(value):
    centred = value - jnp.mean(value, axis=-1, keepdims=True)
    return centred * lax.rsqrt(jnp.mean(centred * centred, axis=-1, keepdims=True) + EPSILON)


def split(value):
    high = value.astype(BF16)
    return high, (value - high.astype(F32)).astype(BF16)


def sigmas(step):
    now = 1.5 * 0.65**step
    return now, 1.5 * 0.65 ** (step + 1), 1.4 * now


def kernel(
    half,
    pair_hbm, bins_ref, tok_ref, atom_ref, owner_ref, coords_ref, noise_ref,
    gate_ref, up_ref, down_ref, proj_ref, binb_ref,
    wq_hbm, wk_hbm, wv_hbm, wg_hbm, wo_hbm,
    cin_ref, lift_ref, tdown_ref, aq_ref, ak_ref, av_ref, ao_ref, wbias_ref, cout_ref,
    coords_out, state_out,
    pair_buf, w_buf, bias_buf, lift_w, down_t, proj_t, centre, bin_pad,
    tok_all, mean_all, mean_own, x_buf, part_o, part_s,
    kv_buf, q_buf, att_buf, onehot_buf, onehot_t, feat_buf, mid_buf, act_buf,
    noisy_buf, noise8, wide_out, lift2,
    pair_sem, w_sem, tok_send, tok_recv, mean_send, mean_recv,
    part_send, part_recv, halo_send, halo_recv,
):
    tokens, columns = bins_ref.shape
    atoms = atom_ref.shape[0]
    me = lax.axis_index("wide")
    side = lax.axis_index("narrow")
    wide = 2 * half
    group = me // half
    place = me - group * half
    own_group = group == side
    is_self = jnp.where(own_group, 1, 0)
    left = lax.rem(me + wide - 1, wide)
    right = lax.rem(me + 1, wide)

    barrier = pltpu.get_barrier_semaphore()

    def each_partner(act):
        def body(r, carry):
            @pl.when(jnp.logical_not(jnp.logical_and(own_group, r == place)))
            def _():
                act(r, (side * half + r, group))
            return carry
        lax.fori_loop(0, half, body, 0)

    each_partner(lambda r, to: pl.semaphore_signal(barrier, inc=1, device_id=to, device_id_type=MESH))
    for to in ((me, 1 - side), (left, side), (right, side)):
        pl.semaphore_signal(barrier, inc=1, device_id=to, device_id_type=MESH)

    def pair_copy(i):
        return pltpu.make_async_copy(pair_hbm.at[i], pair_buf.at[i], pair_sem.at[i])

    def start_pair(i, carry):
        pair_copy(i).start()
        return carry

    lax.fori_loop(0, tokens, start_pair, 0)
    weights = (wq_hbm, wk_hbm, wv_hbm, wg_hbm, wo_hbm)

    def weight_copy(k):
        return pltpu.make_async_copy(weights[k], w_buf.at[k], w_sem.at[k])

    for k in range(5):
        weight_copy(k).start()

    owner = owner_ref[...]
    onehot = (iota((tokens, atoms), 0) == owner).astype(F32)
    onehot_buf[...] = onehot.astype(BF16)
    counts = jnp.sum(onehot, axis=1, keepdims=True)
    flipped = jnp.transpose(onehot)
    onehot_t[...] = jnp.concatenate([flipped, flipped], axis=1).astype(BF16)
    tok_base = tok_ref[...].astype(F32)
    noise8[...] = jnp.zeros_like(noise8)
    noisy_buf[...] = jnp.zeros_like(noisy_buf)
    for step in range(STEPS):
        noise8[step, 0:3, :] = noise_ref[step]
    noisy_buf[0:3, :] = coords_ref[...]
    wide_out[...] = jnp.zeros_like(wide_out)
    wide_out[0:3, :] = cout_ref[...].astype(F32)
    lift_high, lift_low = split(lift_ref[...])
    lift2[0:C_ATOM, :] = lift_high
    lift2[C_ATOM : 2 * C_ATOM, :] = lift_low

    def prepare(step, coords):
        now, _, hat = sigmas(step)
        noisy = coords + now * math.sqrt(0.96) * noise8[step]
        noisy_buf[...] = noisy
        columns_of = jnp.transpose(noisy / math.sqrt(hat * hat + 1.0))
        feat = atom_ref[...].astype(F32)
        for k in range(3):
            feat = feat + columns_of[:, k : k + 1] * cin_ref[k : k + 1, :]
        feat_buf[...] = feat
        pooled = nn(onehot_buf[...], jnp.maximum(feat, 0.0).astype(BF16))
        mean_own[step] = (pooled / counts).astype(BF16)
        act_buf[...] = tok_base + jnp.dot(pooled, lift_ref[...], precision=HIGHEST) / counts

    def mean_copy(step, to):
        return pltpu.make_async_remote_copy(
            src_ref=mean_own.at[step],
            dst_ref=mean_all.at[step, place],
            send_sem=mean_send.at[step],
            recv_sem=mean_recv.at[step],
            device_id=to,
            device_id_type=MESH,
        )

    def send_mean(step):
        each_partner(lambda r, to: mean_copy(step, to).start())

        @pl.when(own_group)
        def _():
            pltpu.make_async_copy(
                mean_own.at[step], mean_all.at[step, place], mean_recv.at[step]
            ).start()

    def wait_all(buffer, send_sem, recv_sem):
        pltpu.make_async_copy(buffer, buffer, recv_sem).wait()

        @pl.when(own_group)
        def _():
            most = buffer.at[pl.ds(0, half - 1)]
            pltpu.make_async_copy(most, most, send_sem).wait()

        @pl.when(jnp.logical_not(own_group))
        def _():
            pltpu.make_async_copy(buffer, buffer, send_sem).wait()

    prepare(0, noisy_buf[...])

    ends = jnp.transpose(gate_ref[...].astype(F32)) * 0.5
    ups = jnp.transpose(up_ref[...].astype(F32))
    for k in range(FF_Z // 8):
        lift_w[16 * k : 16 * k + 16, :] = jnp.concatenate(
            [ends[8 * k : 8 * k + 8, :], ups[8 * k : 8 * k + 8, :]], axis=0
        ).astype(BF16)
    down = down_ref[...].astype(F32)
    down = down - jnp.mean(down, axis=1, keepdims=True)
    down_t[...] = jnp.transpose(down).astype(BF16)
    proj_t[...] = lax.dot_general(
        proj_ref[...],
        (iota((CZ, CZ), 0) == iota((CZ, CZ), 1)).astype(BF16),
        (((0,), (0,)), ((), ())),
        preferred_element_type=F32,
    ).astype(BF16)
    centre[...] = (
        (iota((CZ, CZ), 0) == iota((CZ, CZ), 1)).astype(F32) - 1.0 / CZ
    ).astype(BF16)
    bin_pad[...] = jnp.zeros_like(bin_pad)
    bin_pad[:, 0:NBIN] = binb_ref[...]

    pl.semaphore_wait(barrier, half + 3 - is_self)

    def tok_copy(to):
        return pltpu.make_async_remote_copy(
            src_ref=tok_ref,
            dst_ref=tok_all.at[place],
            send_sem=tok_send,
            recv_sem=tok_recv,
            device_id=to,
            device_id_type=MESH,
        )

    each_partner(lambda r, to: tok_copy(to).start())

    @pl.when(own_group)
    def _():
        pltpu.make_async_copy(tok_ref, tok_all.at[place], tok_recv).start()

    send_mean(0)

    def pair_tile(i, start):
        span = pl.ds(start, PAIR_COLS)
        centred = nt(centre[...], pair_buf[i, span, :])
        spread = lax.rsqrt(jnp.mean(centred * centred, axis=0, keepdims=True) + EPSILON)
        lifted = nn(lift_w[...], (centred * spread).astype(BF16))
        lifted = lifted.reshape(FF_Z // 8, 16, PAIR_COLS)
        lift_a = lifted[:, 0:8, :].reshape(FF_Z, PAIR_COLS)
        lift_b = lifted[:, 8:16, :].reshape(FF_Z, PAIR_COLS)
        hidden = ((lift_a + lift_a * jnp.tanh(lift_a)) * lift_b).astype(BF16)
        cond = centred + nn(down_t[...], hidden)
        spread = lax.rsqrt(jnp.mean(cond * cond, axis=0, keepdims=True) + EPSILON)
        planes = nn(proj_t[...], cond.astype(BF16)) * spread
        bins = bins_ref[pl.ds(i, 1), span]
        table = bin_pad[...]
        for k in range(PAIR_COLS // 128):
            lanes = slice(128 * k, 128 * k + 128)
            index = jnp.broadcast_to(bins[:, lanes], (HEADS, 128))
            level = jnp.take_along_axis(table, index, axis=1)
            bias_buf[pl.ds(pl.multiple_of(i * HEADS, HEADS), HEADS), start + 128 * k : start + 128 * k + 128] = (
                planes[:, lanes] + level
            )

    def pair_row(i, carry):
        pair_copy(i).wait()
        for start in range(0, columns, PAIR_COLS):
            pair_tile(i, start)
        return carry

    lax.fori_loop(0, tokens, pair_row, 0)

    for k in range(5):
        weight_copy(k).wait()
    wait_all(tok_all, tok_send, tok_recv)

    head_mask = (iota((HEADS, D_TOK), 1) // HEAD_DIM == iota((HEADS, D_TOK), 0)).astype(F32)
    lane_mask = (iota((HEADS, 128), 1) == iota((HEADS, 128), 0)).astype(F32)
    expand = (iota((128, D_TOK), 1) // HEAD_DIM == iota((128, D_TOK), 0)).astype(F32)
    chunk_tokens = 8
    chunk_rows = chunk_tokens * HEADS

    def part_copies(step):
        return [
            pltpu.make_async_remote_copy(
                src_ref=ref.at[step, side],
                dst_ref=ref.at[step, side],
                send_sem=part_send.at[step, k],
                recv_sem=part_recv.at[step, k],
                device_id=(me, 1 - side),
                device_id_type=MESH,
            )
            for k, ref in enumerate((part_o, part_s))
        ]

    def halo_copies(step):
        first = kv_buf.at[step, pl.ds(RIM, RIM)]
        last = kv_buf.at[step, pl.ds(atoms, RIM)]
        to_left = pltpu.make_async_remote_copy(
            src_ref=first,
            dst_ref=kv_buf.at[step, pl.ds(atoms + RIM, RIM)],
            send_sem=halo_send.at[step, 0],
            recv_sem=halo_recv.at[step, 0],
            device_id=(left, side),
            device_id_type=MESH,
        )
        to_right = pltpu.make_async_remote_copy(
            src_ref=last,
            dst_ref=kv_buf.at[step, pl.ds(0, RIM)],
            send_sem=halo_send.at[step, 1],
            recv_sem=halo_recv.at[step, 1],
            device_id=(right, side),
            device_id_type=MESH,
        )
        return to_left, to_right

    def attend_tokens(step):
        normed = layer_norm(act_buf[...]).astype(BF16)
        queries = nn(normed, w_buf[0]).astype(BF16).astype(F32)
        spread_q = (queries[:, None, :] * head_mask[None, :, :]).reshape(tokens * HEADS, D_TOK)
        mixed_q = (nt(spread_q.astype(BF16), w_buf[1]) * (1.0 / math.sqrt(HEAD_DIM))).astype(BF16)
        gate_open = jax.nn.sigmoid(nn(normed, w_buf[3]))
        wait_all(mean_all.at[step], mean_send.at[step], mean_recv.at[step])
        per = 4
        for b in range(0, half, per):
            rows = per * tokens
            mean = mean_all[step, b : b + per].reshape(rows, C_ATOM)
            act = tok_all[b : b + per].reshape(rows, D_TOK).astype(F32) + nn(
                jnp.concatenate([mean, mean], axis=1), lift2[...]
            )
            x_buf[b * tokens : b * tokens + rows, :] = layer_norm(act).astype(BF16)
        outs, stat_m, stat_l = [], [], []
        for c in range(tokens // chunk_tokens):
            rows = slice(c * chunk_rows, (c + 1) * chunk_rows)
            scores = nt(mixed_q[rows], x_buf[...]) + bias_buf[rows, :]
            row_max = jnp.max(scores, axis=1, keepdims=True)
            exponents = jnp.exp(scores - row_max)
            row_sum = jnp.sum(exponents, axis=1, keepdims=True)
            mixed = nn(exponents.astype(BF16), x_buf[...]).astype(BF16)
            heads = nn(mixed, w_buf[2]).reshape(chunk_tokens, HEADS, D_TOK)
            outs.append(jnp.sum(heads * head_mask[None], axis=1))
            stat_m.append(
                jnp.sum(row_max.reshape(chunk_tokens, HEADS, 1) * lane_mask[None], axis=1)
            )
            stat_l.append(
                jnp.sum(row_sum.reshape(chunk_tokens, HEADS, 1) * lane_mask[None], axis=1)
            )
        part_o[step, side] = jnp.concatenate(outs, axis=0).astype(BF16)
        part_s[step, side, 0:tokens, :] = jnp.concatenate(stat_m, axis=0)
        part_s[step, side, tokens : 2 * tokens, :] = jnp.concatenate(stat_l, axis=0)
        copies = part_copies(step)
        for copy in copies:
            copy.start()
        for copy in copies:
            copy.wait()
        max_0, max_1 = part_s[step, 0, 0:tokens, :], part_s[step, 1, 0:tokens, :]
        sum_0 = part_s[step, 0, tokens : 2 * tokens, :]
        sum_1 = part_s[step, 1, tokens : 2 * tokens, :]
        top = jnp.maximum(max_0, max_1)
        share_0, share_1 = jnp.exp(max_0 - top), jnp.exp(max_1 - top)
        total = share_0 * sum_0 + share_1 * sum_1
        heads_only = iota((tokens, 128), 1) < HEADS
        total = jnp.where(heads_only, total, 1.0)
        factors = jnp.dot(
            jnp.concatenate([share_0 / total, share_1 / total], axis=0), expand, precision=HIGHEST
        )
        merged = (
            factors[0:tokens] * part_o[step, 0].astype(F32)
            + factors[tokens : 2 * tokens] * part_o[step, 1].astype(F32)
        )
        gated = (merged * gate_open).astype(BF16)
        act_buf[...] = act_buf[...] + nn(gated, w_buf[4])

    def window(step, n, mask):
        start = pl.multiple_of(n * QWIN, QWIN)
        query = q_buf[pl.ds(start, QWIN), :]
        keys = kv_buf[step, pl.ds(start, KWIN), 0:C_ATOM]
        values = kv_buf[step, pl.ds(start, KWIN), C_ATOM : 2 * C_ATOM]
        head_of = iota((QWIN, C_ATOM), 1) // ATOM_DIM
        zero = jnp.zeros_like(query)
        spread_q = jnp.concatenate(
            [jnp.where(head_of == g, query, zero) for g in range(ATOM_HEADS)], axis=0
        )
        scores = nt(spread_q, keys) * (1.0 / math.sqrt(ATOM_DIM)) + wbias_ref[...]
        if mask:
            place_at = n * QWIN + iota((ATOM_HEADS * QWIN, KWIN), 1)
            low = jnp.where(me == 0, RIM, 0)
            high = jnp.where(me == wide - 1, atoms + RIM, atoms + 2 * RIM)
            valid = jnp.logical_and(place_at >= low, place_at < high)
            scores = jnp.where(valid, scores, MASKED_SCORE)
        row_max = jnp.max(scores, axis=1, keepdims=True)
        exponents = jnp.exp(scores - row_max)
        row_sum = jnp.sum(exponents, axis=1, keepdims=True)
        mixed = nn(exponents.astype(BF16), values) / row_sum
        out = jnp.zeros((QWIN, C_ATOM), F32)
        for g in range(ATOM_HEADS):
            out = jnp.where(head_of == g, mixed[g * QWIN : (g + 1) * QWIN], out)
        att_buf[pl.ds(start, QWIN), :] = out.astype(BF16)

    def move_atoms(step):
        now, after, hat = sigmas(step)
        down_normed = layer_norm(act_buf[...]).astype(BF16)
        feed = nn(down_normed, tdown_ref[...])
        feed_high, feed_low = split(feed)
        mid = feat_buf[...] + nn(onehot_t[...], jnp.concatenate([feed_high, feed_low], axis=0))
        mid_buf[...] = mid
        normed = layer_norm(mid).astype(BF16)
        q_buf[...] = nn(normed, aq_ref[...]).astype(BF16)
        kv_buf[step, RIM : RIM + atoms, 0:C_ATOM] = nn(normed, ak_ref[...]).astype(BF16)
        kv_buf[step, RIM : RIM + atoms, C_ATOM : 2 * C_ATOM] = nn(normed, av_ref[...]).astype(BF16)
        copies = halo_copies(step)
        for copy in copies:
            copy.start()
        count = atoms // QWIN
        per = 4

        def several(g, carry):
            for k in range(per):
                window(step, 2 + g * per + k, False)
            return carry

        lax.fori_loop(0, (count - 4) // per, several, 0)
        for copy in copies:
            copy.wait()
        for n in (0, 1, count - 2, count - 1):
            window(step, n, True)
        final = mid_buf[...] + nn(att_buf[...], ao_ref[...])
        final_normed = layer_norm(final).astype(BF16)
        update = nt(wide_out[...].astype(BF16), final_normed)[0:8]
        noisy = noisy_buf[...]
        denoised = noisy / (hat * hat + 1.0) + hat / math.sqrt(hat * hat + 1.0) * update
        return noisy + 1.5 * (after - hat) / hat * (noisy - denoised)

    for step in range(STEPS):
        attend_tokens(step)
        coords = move_atoms(step)
        if step + 1 < STEPS:
            prepare(step + 1, coords)
            send_mean(step + 1)
    coords_out[...] = coords[0:3, :]
    state_out[...] = act_buf[...].astype(BF16)


def local(
    pair_rep, pair_bins, token_single, atom_single, atom_token, init_coords, coord_noise,
    pair_gate, pair_up, pair_down, bias_proj, bin_bias,
    token_query, token_key, token_value, token_gate, token_out,
    coord_in, atom_lift, token_down, atom_query, atom_key, atom_value, atom_out,
    window_bias, coord_out,
):
    half = lax.axis_size("wide") // 2
    tokens, columns = pair_bins.shape
    atoms = atom_single.shape[1]
    anywhere = pl.BlockSpec(memory_space=pl.ANY)
    near = pl.BlockSpec(memory_space=pltpu.VMEM)
    in_specs = [anywhere] + [near] * 11 + [anywhere] * 5 + [near] * 9
    scratch = [
        pltpu.VMEM((tokens, columns, CZ), BF16),
        pltpu.VMEM((5, D_TOK, D_TOK), BF16),
        pltpu.VMEM((tokens * HEADS, columns), F32),
        pltpu.VMEM((2 * FF_Z, CZ), BF16),
        pltpu.VMEM((CZ, FF_Z), BF16),
        pltpu.VMEM((HEADS, CZ), BF16),
        pltpu.VMEM((CZ, CZ), BF16),
        pltpu.VMEM((HEADS, 128), F32),
        pltpu.VMEM((half, tokens, D_TOK), BF16),
        pltpu.VMEM((STEPS, half, tokens, C_ATOM), BF16),
        pltpu.VMEM((STEPS, tokens, C_ATOM), BF16),
        pltpu.VMEM((half * tokens, D_TOK), BF16),
        pltpu.VMEM((STEPS, 2, tokens, D_TOK), BF16),
        pltpu.VMEM((STEPS, 2, 2 * tokens, 128), F32),
        pltpu.VMEM((STEPS, atoms + 2 * RIM, 2 * C_ATOM), BF16),
        pltpu.VMEM((atoms, C_ATOM), BF16),
        pltpu.VMEM((atoms, C_ATOM), BF16),
        pltpu.VMEM((tokens, atoms), BF16),
        pltpu.VMEM((atoms, 2 * tokens), BF16),
        pltpu.VMEM((atoms, C_ATOM), F32),
        pltpu.VMEM((atoms, C_ATOM), F32),
        pltpu.VMEM((tokens, D_TOK), F32),
        pltpu.VMEM((8, atoms), F32),
        pltpu.VMEM((STEPS, 8, atoms), F32),
        pltpu.VMEM((16, C_ATOM), F32),
        pltpu.VMEM((2 * C_ATOM, D_TOK), BF16),
        pltpu.SemaphoreType.DMA((tokens,)),
        pltpu.SemaphoreType.DMA((5,)),
        pltpu.SemaphoreType.DMA,
        pltpu.SemaphoreType.DMA,
        pltpu.SemaphoreType.DMA((STEPS,)),
        pltpu.SemaphoreType.DMA((STEPS,)),
        pltpu.SemaphoreType.DMA((STEPS, 2)),
        pltpu.SemaphoreType.DMA((STEPS, 2)),
        pltpu.SemaphoreType.DMA((STEPS, 2)),
        pltpu.SemaphoreType.DMA((STEPS, 2)),
    ]

    def body(*refs):
        kernel(half, *refs)

    coords, state = pl.pallas_call(
        body,
        out_shape=(
            jax.ShapeDtypeStruct((3, atoms), F32),
            jax.ShapeDtypeStruct((tokens, D_TOK), BF16),
        ),
        in_specs=in_specs,
        out_specs=(near, near),
        scratch_shapes=scratch,
        compiler_params=pltpu.CompilerParams(collective_id=0, has_side_effects=True),
        name="denoise",
    )(
        pair_rep, pair_bins, token_single, atom_single[0], atom_token, init_coords[:, 0, :],
        coord_noise[:, :, 0, :], pair_gate, pair_up, pair_down, bias_proj, bin_bias,
        token_query, token_key, token_value, token_gate, token_out, coord_in, atom_lift,
        token_down, atom_query, atom_key, atom_value, atom_out,
        window_bias.reshape(ATOM_HEADS * QWIN, KWIN), coord_out,
    )
    return coords[:, None, :], state


def solution(mesh):
    placed = (
        P("wide", "narrow", None),
        P("wide", "narrow"),
        P("wide", None),
        P("wide", None, None),
        P("wide", None),
        P(None, "wide", None),
        P(None, None, "wide", None),
    ) + (P(),) * 19
    return jax.shard_map(
        local,
        mesh=mesh,
        in_specs=placed,
        out_specs=(P(None, "wide", None), P("wide", None)),
        check_vma=False,
    )
```

time: 514 us -> 143 us (0.28); the launches traced: 508 us -> 143 us
  waiting for transfers between devices: 254 us -> 0 us
  Pallas kernels: 0 us -> 135 us
  matrix products: 132 us -> 0 us
  local copies, waits for them, and re-layouts: 63.8 us -> 6.78 us
  other arithmetic: 33 us -> 0 us
  between operations: 14.7 us -> 0.64 us
  starting transfers between devices: 9.51 us -> 0 us
    all_gather x5 -> x0, waiting for transfers between devices: 252 us -> none  [the longest x2 128 us: local(): lax.all_gather(value_rows, 'wide', axis=0, tiled=True)]
    pallas_call x0 -> x1, Pallas kernels: none -> 135 us  [local(): pl.pallas_call(body, out_shape=(jax.ShapeDtypeStruct((3, atoms), F32), ja...]
    dot_general x68 -> x0, matrix products: 132 us -> none  [the longest x8 41 us: pair_block_bias(): jnp.einsum('rcf,fk->rck', hidden, pair_down, preferred_element_type=jnp.f...]
    reduce_sum x36 -> x0, other arithmetic: 30.4 us -> none  [the longest x23 15.3 us: layer_norm(): jnp.mean(centred * centred, axis=-1, keepdims=True) + EPSILON]
    all_gather x4 -> x0, local copies, waits for them, and re-layouts: 18.9 us -> none  [the longest x2 9.52 us: local(): lax.all_gather(value_rows, 'wide', axis=0, tiled=True)]
    unnamed x93 -> x5, local copies, waits for them, and re-layouts: 20.3 us -> 6.17 us
    squeeze x4 -> x1, local copies, waits for them, and re-layouts: 11.3 us -> 0.61 us  [local(): coord_noise[:, :, 0, :]]
    ppermute x4 -> x0, starting transfers between devices: 8.87 us -> none  [the longest x2 4.79 us: extended(): lax.ppermute(lax.slice_in_dim(block, 0, width, axis=dim), axis, backward)]
  transfers between devices with their start and end apart: 9 -> 0, of which waited for: 6 -> 0; matrix products, arithmetic and copies ran while one was open for 31% -> 0% of each run, Pallas kernels for 0% -> 0%
where the time goes in v1:
time: 143 us
  Pallas kernels  135 us (94%)
  local copies, waits for them, and re-layouts  6.78 us (5%)
    pallas_call x1, Pallas kernels, local(): pl.pallas_call(body, out_shape=(jax.ShapeDtypeStruct((3, atoms), F32), ja...  135 us
    unnamed x5, local copies, waits for them, and re-layouts  6.17 us

profile of v1, /device:TPU:1, one launch (start us, length us, event | category | flops | bytes accessed | tf_op | source)
XLA Modules:
  0.0 142.6 jit_solution(6031257238106205106)
XLA Ops:
  0.6 1.3 copy.38
  1.9 0.7 copy.37
  2.7 0.6 copy.31.refs_6_
  3.3 1.4 copy.32.refs_10_
  4.7 135.2 %denoise.1 = (f32[3,768]{1,0:T(4,128)}, bf16[32,768]{1,0:T(8,128)(2,1)}) custom-call(bf16[32,1024,128]{2,1,0:T(8,128)(2,1)} %refs_0_.1, s32[32,1024]{1,0:T(8,128)} %refs_1_.1, bf16[32,768]{1,0:T(8,128)(2,1)} %refs_2_.1, bf16[768,128]{1,0:T(8,128)(2,1)} %bitcast.9, s32[1,768]{1,0:T(1,128)} %refs_4_.1, f32[3,768]{1,0:T(4,128)} %bitcast.12, ...), custom_call_target="tpu_custom_call" | custom-call | tf_op jit(solution)/shard_map/denoise/pallas_call | solution.py:477
  139.9 1.3 copy.33
  141.2 1.4 copy.40
